TPU v7x, 32 devices: a whole 2x2x4 slice. The times are simulated.
32 devices in a mesh: dp: 2 (over y), seq: 16 (over z, x, core).
Axes of the slice: x: 2, y: 2, z: 4, core: 2. Of those that a mesh axis runs over, the one named last changes fastest.
Arguments:
- layer_input: bfloat16 [4096, 1024], P(('dp', 'seq')), may hold values from -6 to 6
- norm_gain: bfloat16 [1024], P('dp'), may hold values from 0.5 to 1.5
- in_weight: bfloat16 [1024, 4384], P('dp'), may hold values from -0.1875 to 0.1875
- conv_weight: bfloat16 [4, 2304], P(None, 'dp'), may hold values from -3 to 3
- conv_bias: bfloat16 [2304], P('dp'), may hold values from -2 to 2
- step_bias: bfloat16 [32], P('dp'), may hold values from -5 to -1
- rate_log: bfloat16 [32], P('dp'), may hold values from -4 to 2
- skip_gain: bfloat16 [32], P('dp'), may hold values from 0.5 to 2
- gate_gain: bfloat16 [2048], P('dp'), may hold values from 0.5 to 1.5
- out_weight: bfloat16 [2048, 1024], P('dp'), may hold values from -0.125 to 0.125
- cotangent: bfloat16 [4096, 1024], P(('dp', 'seq')), may hold values from -6 to 6
Outputs:
- layer_output: bfloat16 [4096, 1024], P(('dp', 'seq'))
- input_grad: float32 [4096, 1024], P(('dp', 'seq'))
- norm_gain_grad: float32 [1024], P('dp')
- in_weight_grad: float32 [1024, 4384], P('dp')
- conv_weight_grad: float32 [4, 2304], P(None, 'dp')
- conv_bias_grad: float32 [2304], P('dp')
- step_bias_grad: float32 [32], P('dp')
- rate_log_grad: float32 [32], P('dp')
- skip_gain_grad: float32 [32], P('dp')
- gate_gain_grad: float32 [2048], P('dp')
- out_weight_grad: float32 [2048, 1024], P('dp')
All inputs are finite; a program needn't handle non-finite values.
Results may differ from a plain program's by a relative error of at most 0.012.
Values may be sent and summed in bfloat16 or wider, within the bound.
No kernel may reach another device: no remote copies, remote signals or barrier semaphores. Data moves between devices by JAX's collectives and lax.ppermute only.
A program may use at most 192 MiB of HBM per device.

v0:
```python
import jax
import jax.numpy as jnp
from jax import lax
from jax.sharding import PartitionSpec as P

BLOCK = 256
epsilon = 1e-05
highest = lax.Precision.HIGHEST


def front_norm(values, gain):
    scale = lax.rsqrt(jnp.mean(values * values, axis=-1, keepdims=True) + epsilon)
    return values * scale * gain


def gated_norm(mixer_out, gate_in, gain):
    gated = mixer_out * jax.nn.silu(gate_in)
    scale = lax.rsqrt(jnp.mean(gated * gated, axis=-1, keepdims=True) + epsilon)
    return gated * scale * gain


def causal_conv(values, taps, offset):
    width = taps.shape[0]
    length = values.shape[0]
    padded = jnp.concatenate(
        [jnp.zeros((width - 1, values.shape[1]), values.dtype), values], axis=0
    )
    total = offset[None, :] + jnp.zeros_like(values)
    for index in range(width):
        total = total + taps[index][None, :] * padded[index : index + length]
    return jax.nn.silu(total)


def scan_blocks(values, steps, rates, keys, queries):
    length, heads, hdim = values.shape
    states = keys.shape[1]
    blocks = length // BLOCK
    items = (
        values.reshape(blocks, BLOCK, heads, hdim),
        steps.reshape(blocks, BLOCK, heads),
        keys.reshape(blocks, BLOCK, states),
        queries.reshape(blocks, BLOCK, states),
    )

    def one_block(state, item):
        val_blk, step_blk, key_blk, query_blk = item
        logs = (step_blk * rates[None, :]).T
        cums = jnp.cumsum(logs, axis=1)
        rows = lax.broadcasted_iota(jnp.int32, (BLOCK, BLOCK), 0)
        cols = lax.broadcasted_iota(jnp.int32, (BLOCK, BLOCK), 1)
        lower = (rows >= cols)[None]
        spread = cums[:, :, None] - cums[:, None, :]
        decay = jnp.where(lower, jnp.exp(jnp.where(lower, spread, 0.0)), 0.0)
        scores = jnp.dot(query_blk, key_blk.T, precision=highest)
        weights = scores[None] * decay * step_blk.T[:, None, :]
        inside = jnp.einsum("hts,shp->thp", weights, val_blk, precision=highest)
        carried = (
            jnp.einsum("tn,hpn->thp", query_blk, state, precision=highest)
            * jnp.exp(cums).T[:, :, None]
        )
        tail = jnp.exp(cums[:, -1:] - cums) * step_blk.T
        update = jnp.einsum("hs,shp,sn->hpn", tail, val_blk, key_blk, precision=highest)
        fresh = state * jnp.exp(cums[:, -1])[:, None, None] + update
        return (fresh, inside + carried)

    start = jnp.zeros((heads, hdim, states), jnp.float32)
    final_state, outputs = lax.scan(jax.checkpoint(one_block), start, items)
    return outputs.reshape(length, heads, hdim)


def mixer(
    x_head, step_raw, key_query, x_taps, x_offset, kq_taps, kq_offset, step_shift, rate_logs, skips
):
    x_conv = causal_conv(x_head, x_taps, x_offset)
    kq_conv = causal_conv(key_query, kq_taps, kq_offset)
    states = kq_conv.shape[1] // 2
    keys = kq_conv[:, :states]
    queries = kq_conv[:, states:]
    steps = jax.nn.softplus(step_raw + step_shift[None, :])
    rates = -jnp.exp(rate_logs)
    heads = step_shift.shape[0]
    length = x_head.shape[0]
    values = x_conv.reshape(length, heads, -1)
    mixed = scan_blocks(values, steps, rates, keys, queries) + values * skips[None, :, None]
    return mixed.reshape(length, -1)


def own_block(values, dim):
    parts = lax.axis_size("dp")
    width = values.shape[dim] // parts
    return lax.dynamic_slice_in_dim(values, lax.axis_index("dp") * width, width, dim)


def local(
    layer_input,
    norm_gain,
    in_weight,
    conv_weight,
    conv_bias,
    step_bias,
    rate_log,
    skip_gain,
    gate_gain,
    out_weight,
    cotangent,
):
    (
        full_gain,
        full_in,
        full_taps,
        full_offset,
        full_shift,
        full_rates,
        full_skip,
        full_gate,
        full_out,
    ) = (
        lax.all_gather(norm_gain, "dp", axis=0, tiled=True),
        lax.all_gather(in_weight, "dp", axis=0, tiled=True),
        lax.all_gather(conv_weight, "dp", axis=1, tiled=True),
        lax.all_gather(conv_bias, "dp", axis=0, tiled=True),
        lax.all_gather(step_bias, "dp", axis=0, tiled=True),
        lax.all_gather(rate_log, "dp", axis=0, tiled=True),
        lax.all_gather(skip_gain, "dp", axis=0, tiled=True),
        lax.all_gather(gate_gain, "dp", axis=0, tiled=True),
        lax.all_gather(out_weight, "dp", axis=0, tiled=True),
    )
    inner = full_out.shape[0]
    heads = full_shift.shape[0]
    states = (full_taps.shape[1] - inner) // 2
    group = lax.axis_size("seq")
    local_heads = heads // group
    span = local_heads * (inner // heads)
    rank = lax.axis_index("seq")
    tok_vals = layer_input.astype(jnp.float32)
    normed, pull_front = jax.vjp(front_norm, tok_vals, full_gain.astype(jnp.float32))
    normed_low = normed.astype(jnp.bfloat16)
    proj_low = jnp.dot(normed_low, full_in, preferred_element_type=jnp.float32).astype(jnp.bfloat16)
    gate_in = proj_low[:, :inner]
    x_part = proj_low[:, inner : 2 * inner]
    kq_part = proj_low[:, 2 * inner : 2 * inner + 2 * states]
    step_part = proj_low[:, 2 * inner + 2 * states :]
    x_head, step_head = (
        lax.all_to_all(x_part, "seq", split_axis=1, concat_axis=0, tiled=True),
        lax.all_to_all(step_part, "seq", split_axis=1, concat_axis=0, tiled=True),
    )
    kq_whole = lax.all_gather(kq_part, "seq", axis=0, tiled=True)
    taps_f = full_taps.astype(jnp.float32)
    offset_f = full_offset.astype(jnp.float32)
    x_taps = lax.dynamic_slice_in_dim(taps_f, rank * span, span, 1)
    x_offset = lax.dynamic_slice_in_dim(offset_f, rank * span, span, 0)
    shift_own = lax.dynamic_slice_in_dim(
        full_shift.astype(jnp.float32), rank * local_heads, local_heads, 0
    )
    rates_own = lax.dynamic_slice_in_dim(
        full_rates.astype(jnp.float32), rank * local_heads, local_heads, 0
    )
    skip_own = lax.dynamic_slice_in_dim(
        full_skip.astype(jnp.float32), rank * local_heads, local_heads, 0
    )
    mixed, pull_mix = jax.vjp(
        mixer,
        x_head.astype(jnp.float32),
        step_head.astype(jnp.float32),
        kq_whole.astype(jnp.float32),
        x_taps,
        x_offset,
        taps_f[:, inner:],
        offset_f[inner:],
        shift_own,
        rates_own,
        skip_own,
    )
    mixer_tok = lax.all_to_all(
        mixed.astype(jnp.bfloat16), "seq", split_axis=0, concat_axis=1, tiled=True
    )
    gate_out, pull_gate = jax.vjp(
        gated_norm,
        mixer_tok.astype(jnp.float32),
        gate_in.astype(jnp.float32),
        full_gate.astype(jnp.float32),
    )
    gate_low = gate_out.astype(jnp.bfloat16)
    layer_output = (
        tok_vals + jnp.dot(gate_low, full_out, preferred_element_type=jnp.float32)
    ).astype(jnp.bfloat16)
    out_grad = jnp.dot(gate_low.T, cotangent, preferred_element_type=jnp.float32)
    d_gate_out = jnp.dot(cotangent, full_out.T, preferred_element_type=jnp.float32)
    d_mixer_tok, d_gate_in, gate_grad = pull_gate(d_gate_out)
    d_mixer_head = lax.all_to_all(
        d_mixer_tok.astype(jnp.bfloat16), "seq", split_axis=1, concat_axis=0, tiled=True
    )
    (
        d_x_head,
        d_step_head,
        d_kq_whole,
        d_x_taps,
        d_x_offset,
        d_kq_taps,
        d_kq_offset,
        d_shift_own,
        d_rates_own,
        d_skip_own,
    ) = pull_mix(d_mixer_head.astype(jnp.float32))
    d_x_tok, d_step_tok = (
        lax.all_to_all(
            d_x_head.astype(jnp.bfloat16), "seq", split_axis=0, concat_axis=1, tiled=True
        ),
        lax.all_to_all(
            d_step_head.astype(jnp.bfloat16), "seq", split_axis=0, concat_axis=1, tiled=True
        ),
    )
    d_kq_tok = lax.psum_scatter(
        d_kq_whole.astype(jnp.bfloat16), "seq", scatter_dimension=0, tiled=True
    )
    d_proj = jnp.concatenate(
        [d_gate_in.astype(jnp.bfloat16), d_x_tok, d_kq_tok, d_step_tok], axis=1
    )
    in_grad = jnp.dot(normed_low.T, d_proj, preferred_element_type=jnp.float32)
    d_normed = jnp.dot(d_proj, full_in.T, preferred_element_type=jnp.float32)
    d_front, gain_grad = pull_front(d_normed)
    input_grad = d_front + cotangent.astype(jnp.float32)
    x_tap_grad = lax.dynamic_update_slice_in_dim(
        jnp.zeros((taps_f.shape[0], inner), jnp.float32), d_x_taps, rank * span, 1
    )
    taps_grad = jnp.concatenate([x_tap_grad, d_kq_taps], axis=1)
    x_off_grad = lax.dynamic_update_slice_in_dim(
        jnp.zeros((inner,), jnp.float32), d_x_offset, rank * span, 0
    )
    offset_grad = jnp.concatenate([x_off_grad, d_kq_offset], axis=0)
    head_zeros = jnp.zeros((heads,), jnp.float32)
    shift_grad = lax.dynamic_update_slice_in_dim(head_zeros, d_shift_own, rank * local_heads, 0)
    rates_grad = lax.dynamic_update_slice_in_dim(head_zeros, d_rates_own, rank * local_heads, 0)
    skip_grad = lax.dynamic_update_slice_in_dim(head_zeros, d_skip_own, rank * local_heads, 0)
    in_part, out_part = (
        lax.psum_scatter(in_grad, ("dp", "seq"), scatter_dimension=0, tiled=True),
        lax.psum_scatter(out_grad, ("dp", "seq"), scatter_dimension=0, tiled=True),
    )
    in_shard, out_shard = (
        lax.all_gather(in_part, "seq", axis=0, tiled=True),
        lax.all_gather(out_part, "seq", axis=0, tiled=True),
    )
    gain_all, taps_all, offset_all, shift_all, rates_all, skip_all, gate_all = lax.psum(
        (gain_grad, taps_grad, offset_grad, shift_grad, rates_grad, skip_grad, gate_grad),
        ("dp", "seq"),
    )
    gain_shard = own_block(gain_all, 0)
    taps_shard = own_block(taps_all, 1)
    offset_shard = own_block(offset_all, 0)
    shift_shard = own_block(shift_all, 0)
    rates_shard = own_block(rates_all, 0)
    skip_shard = own_block(skip_all, 0)
    gate_shard = own_block(gate_all, 0)
    return (
        layer_output,
        input_grad,
        gain_shard,
        in_shard,
        taps_shard,
        offset_shard,
        shift_shard,
        rates_shard,
        skip_shard,
        gate_shard,
        out_shard,
    )


def solution(mesh):
    return jax.shard_map(
        local,
        mesh=mesh,
        in_specs=(
            P(("dp", "seq"), None),
            P("dp"),
            P("dp", None),
            P(None, "dp"),
            P("dp"),
            P("dp"),
            P("dp"),
            P("dp"),
            P("dp"),
            P("dp", None),
            P(("dp", "seq"), None),
        ),
        out_specs=(
            P(("dp", "seq"), None),
            P(("dp", "seq"), None),
            P("dp"),
            P("dp", None),
            P(None, "dp"),
            P("dp"),
            P("dp"),
            P("dp"),
            P("dp"),
            P("dp"),
            P("dp", None),
        ),
        check_vma=False,
    )
```

profile of v0, /device:TPU:0, one launch (start us, length us, event | category | flops | bytes accessed | tf_op | source)
XLA Modules:
  0.0 1092.6 jit_solution(7979534498139653313)
XLA Ops:
  8.0 5.3 all-gather
  13.4 111.9 %all-gather.8.cloned.1.call-done = bf16[1024,4384]{0,1:T(8,128)(2,1)} async-done(((bf16[512,4384]{0,1:T(8,128)(2,1)}), bf16[1024,4384]{0,1:T(8,128)(2,1)}) %all-gather.8.cloned.1.call-update) | async-done | bytes 8978448 | tf_op jit(solution)/shard_map/all_gather | solution.py:119
  125.3 6.1 convolution_convert_fusion
  137.9 5.6 all-to-all-start
  145.6 4.9 all-reduce.26
  157.2 6.5 all-to-all-start.1
  165.2 12.9 %all-to-all-done.1 = bf16[128,16,128]{2,0,1:T(8,128)(2,1)S(1)} async-done(((bf16[128,16,128]{2,0,1:T(8,128)(2,1)}), bf16[128,16,128]{2,0,1:T(8,128)(2,1)S(1)}, u32[]{:S(2)}, u32[]{:S(2)}) %all-to-all-start.1) | async-done | bytes 524320 | tf_op jit(solution)/shard_map/all_to_all | solution.py:144
  195.8 75.2 %while.44 = (s32[]{:T(128)}, f32[2,64,128]{2,1,0:T(8,128)S(1)}, f32[8,256,2,64]{1,3,2,0:T(8,128)}, f32[8,2,64,128]{3,2,1,0:T(8,128)}, f32[8,256,2]{1,2,0:T(2,128...) while((s32[]{:T(128)}, f32[2,64,128]{2,1,0:T(8,128)S(1)}, ...), condition=%wide.region_4.5_spmd.clone.clone, body=%wide.region_1.4_spmd.clone.clone.sunk | while | flops 302892544 | bytes 2142528 | solution.py:67
  280.5 5.1 all-to-all-start.2
  289.9 10.1 all-to-all-done.2
  316.2 13.6 %all-to-all-done.3 = bf16[128,16,128]{2,0,1:T(8,128)(2,1)S(1)} async-done(((bf16[128,16,128]{2,0,1:T(8,128)(2,1)}), bf16[128,16,128]{2,0,1:T(8,128)(2,1)S(1)}, u32[]{:S(2)}, u32[]{:S(2)}) %all-to-all-start.3) | async-done | bytes 524320 | tf_op jit(solution)/shard_map/all_to_all | solution.py:190
  342.0 173.5 %while.43 = (s32[]{:T(128)}, f32[2]{0:T(128)}, f32[2,64,128]{2,1,0:T(8,128)S(1)}, f32[8,256,2,64]{1,3,2,0:T(8,128)}, f32[8,256,2]{1,2,0:T(2,128)}, /*index=5*/f3...) while((s32[]{:T(128)}, f32[2]{0:T(128)}, ...), condition=%wide.region_20.21_spmd.clone, body=%wide.region_7.20_spmd.clone.sunk | while | flops 758179328 | bytes 7921532 | solution.py:67
  529.4 4.7 fusion.131
  551.2 16.4 %all-to-all-done.4 = bf16[16,128,128]{2,1,0:T(8,128)(2,1)S(1)} async-done(((bf16[16,128,128]{2,1,0:T(8,128)(2,1)}), bf16[16,128,128]{2,1,0:T(8,128)(2,1)S(1)}, u32[]{:S(2)}, u32[]{:S(2)}) %all-to-all-start.4) | async-done | bytes 524320 | tf_op jit(solution)/shard_map/all_to_all | solution.py:206
  567.6 5.3 all-to-all-start.5
  573.3 13.9 %reduce-scatter.10.cloned.1.call-done = bf16[128,256]{1,0:T(8,128)(2,1)} async-done(((bf16[2048,256]{1,0:T(8,128)(2,1)}), bf16[128,256]{1,0:T(8,128)(2,1)}) %reduce-scatter.10.cloned.1.call-update) | async-done | bytes 65552
  588.2 8.0 fusion.110
  596.2 141.3 %reduce-scatter.8.cloned.1.call-done = f32[64,1024]{1,0:T(8,128)} async-done(((f32[2048,1024]{1,0:T(8,128)}), f32[64,1024]{1,0:T(8,128)}) %reduce-scatter.8.cloned.1.call-update) | async-done | bytes 262160 | tf_op jit(solution)/shard_map/reduce_scatter | solution.py:237
  737.6 194.8 %reduce-scatter.6.cloned.1.call-done = f32[32,4384]{1,0:T(8,128)} async-done(((f32[1024,4384]{1,0:T(8,128)}), f32[32,4384]{1,0:T(8,128)}) %reduce-scatter.6.cloned.1.call-update) | async-done | bytes 561168 | tf_op jit(solution)/shard_map/reduce_scatter | solution.py:236
  938.3 5.1 fusion.106
  943.4 47.0 %all-reduce.25 = (f32[1024]{0:T(1024)S(1)}, f32[4,2304]{1,0:T(4,128)S(1)}, f32[2304]{0:T(1024)S(1)}, f32[32]{0:T(128)S(1)}, f32[32]{0:T(128)S(1)}, /*index=5*/f32[32]{0:T(128)S(1)}, f32[2048]{0:T(1024)S(1)}) all-reduce(f32[1024]{0:T(1024)S(1)} %get-tuple-element.697, ...), channel_id=1, replica_groups=mesh['dp'=2,'seq'=16] {'dp','seq'}, use_global_device_ids=true, to_apply=%region_24.25 | all-reduce | flops 14688 | bytes 117504 | tf_op jit(solution)/shard_map/psum | solution.py:243
  995.8 75.6 %all-gather.14.cloned.1.call-done = f32[512,4384]{1,0:T(8,128)} async-done(((f32[32,4384]{1,0:T(8,128)}), f32[512,4384]{1,0:T(8,128)}) %all-gather.14.cloned.1.call-update) | async-done | bytes 8978448 | tf_op jit(solution)/shard_map/all_gather | solution.py:240
  1071.4 9.4 copy.130
  1080.8 4.8 copy.253
  (810 shorter events, 366.9 us)
Async XLA Ops:
  7.2 118.1 %all-gather.8.cloned.1.call-start = ((), (), s32[]{:S(2)}) async-start(), calls=%async_computation.9 | async-start | bytes 13467648 | tf_op jit(solution)/shard_map/all_gather | solution.py:119
  7.9 176.3 %all-gather.10.cloned.1.call-start = ((), (), s32[]{:S(2)}) async-start(), calls=%async_computation.10 | async-start | bytes 1114112 | tf_op jit(solution)/shard_map/all_gather | solution.py:147
  13.4 118.0 %copy-start.65 = (f32[128]{0:T(128)}, f32[128]{0:T(128)S(1)}, u32[]{:S(2)}) copy-start(f32[128]{0:T(128)S(1)} %fusion.108) | copy-start | bytes 1540
  13.4 118.0 %copy-start.27 = (f32[128]{0:T(128)}, f32[128]{0:T(128)S(1)}, u32[]{:S(2)}) copy-start(f32[128]{0:T(128)S(1)} %fusion.126) | copy-start | bytes 1540
  131.5 25.7 %copy-start.7 = (bf16[128,4384]{0,1:T(8,128)(2,1)}, bf16[128,4384]{0,1:T(8,128)(2,1)S(1)}, u32[]{:S(2)}) copy-start(bf16[128,4384]{0,1:T(8,128)(2,1)S(1)} %convolution_convert_fusion) | copy-start | bytes 3366916
  132.2 169.8 %all-gather.12.cloned.1.call-start = ((), (), s32[]{:S(2)}) async-start(), calls=%async_computation.11 | async-start | bytes 6291456 | tf_op jit(solution)/shard_map/all_gather | solution.py:126
  137.9 19.3 %all-to-all-start = ((bf16[128,16,2]{0,2,1:T(2,128)(2,1)}), bf16[128,16,2]{0,2,1:T(2,128)(2,1)S(1)}, u32[]{:S(2)}, u32[]{:S(2)}) async-start(bf16[128,16,2]{0,2,1:T(2,128)(2,1)} %bitcast.3), calls=%async_computation | async-start | bytes 16384 | tf_op jit(solution)/shard_map/all_to_all | solution.py:145
  150.5 27.7 %copy-start.69 = (f32[32]{0:T(128)}, f32[32]{0:T(128)S(1)}, u32[]{:S(2)}) copy-start(f32[32]{0:T(128)S(1)} %convert_element_type.120) | copy-start | bytes 388
  157.2 23.7 %copy-start.23 = (bf16[128,16,2]{0,2,1:T(2,128)(2,1)}, bf16[128,16,2]{0,2,1:T(2,128)(2,1)S(1)}, u32[]{:S(2)}) copy-start(bf16[128,16,2]{0,2,1:T(2,128)(2,1)S(1)} %all-to-all-done) | copy-start | bytes 24580
  157.2 20.9 %all-to-all-start.1 = ((bf16[128,16,128]{2,0,1:T(8,128)(2,1)}), bf16[128,16,128]{2,0,1:T(8,128)(2,1)S(1)}, u32[]{:S(2)}, u32[]{:S(2)}) async-start(bf16[128,16,128]{2,0,1:T(8,128)(2,1)} %copy.109), calls=%async_computation.1 | async-start | bytes 1048576 | tf_op jit(solution)/shard_map/all_to_all | solution.py:144
  180.9 97.4 %copy-start.2 = (f32[2048,128]{1,0:T(8,128)}, f32[2048,128]{1,0:T(8,128)S(1)}, u32[]{:S(2)}) copy-start(f32[2048,128]{1,0:T(8,128)S(1)} %get-tuple-element.765) | copy-start | bytes 3145732
  280.5 19.6 %all-to-all-start.2 = ((bf16[16,128,128]{2,1,0:T(8,128)(2,1)}), bf16[16,128,128]{2,1,0:T(8,128)(2,1)S(1)}, u32[]{:S(2)}, u32[]{:S(2)}) async-start(bf16[16,128,128]{2,1,0:T(8,128)(2,1)} %bitcast.20), calls=%async_computation.2 | async-start | bytes 1048576 | tf_op jit(solution)/shard_map/all_to_all | solution.py:174
  311.2 18.6 %all-to-all-start.3 = ((bf16[128,16,128]{2,0,1:T(8,128)(2,1)}), bf16[128,16,128]{2,0,1:T(8,128)(2,1)S(1)}, u32[]{:S(2)}, u32[]{:S(2)}) async-start(bf16[128,16,128]{2,0,1:T(8,128)(2,1)} %copy.118), calls=%async_computation.3 | async-start | bytes 1048576 | tf_op jit(solution)/shard_map/all_to_all | solution.py:190
  315.3 271.9 %reduce-scatter.10.cloned.1.call-start = ((), (), s32[]{:S(2)}) async-start(), calls=%async_computation.16 | async-start | bytes 1114112
  529.1 208.4 %reduce-scatter.8.cloned.1.call-start = ((), (), s32[]{:S(2)}) async-start(), calls=%async_computation.14 | async-start | bytes 8650752 | tf_op jit(solution)/shard_map/reduce_scatter | solution.py:237
  546.2 42.0 %copy-start.14 = (bf16[128,2048]{0,1:T(8,128)(2,1)S(1)}, bf16[128,2048]{0,1:T(8,128)(2,1)}, u32[]{:S(2)}) copy-start(bf16[128,2048]{0,1:T(8,128)(2,1)} %get-tuple-element.779) | copy-start | bytes 1572868
  546.2 42.0 %copy-start.28 = (f32[128]{0:T(128)S(1)}, f32[128]{0:T(128)}, u32[]{:S(2)}) copy-start(f32[128]{0:T(128)} %copy-done.27) | copy-start | bytes 1540
  546.2 21.5 %all-to-all-start.4 = ((bf16[16,128,128]{2,1,0:T(8,128)(2,1)}), bf16[16,128,128]{2,1,0:T(8,128)(2,1)S(1)}, u32[]{:S(2)}, u32[]{:S(2)}) async-start(bf16[16,128,128]{2,1,0:T(8,128)(2,1)} %bitcast.441), calls=%async_computation.4 | async-start | bytes 1048576 | tf_op jit(solution)/shard_map/all_to_all | solution.py:206
  567.6 20.5 %all-to-all-start.5 = ((bf16[16,128,2]{1,2,0:T(2,128)(2,1)}), bf16[16,128,2]{1,2,0:T(2,128)(2,1)S(1)}, u32[]{:S(2)}, u32[]{:S(2)}) async-start(bf16[16,128,2]{1,2,0:T(2,128)(2,1)} %fusion.124), calls=%async_computation.5 | async-start | bytes 16384 | tf_op jit(solution)/shard_map/all_to_all | solution.py:209
  573.0 359.4 %reduce-scatter.6.cloned.1.call-start = ((), (), s32[]{:S(2)}) async-start(), calls=%async_computation.12 | async-start | bytes 18923520 | tf_op jit(solution)/shard_map/reduce_scatter | solution.py:236
  596.2 399.6 %all-gather.16.cloned.1.call-start = ((), (), s32[]{:S(2)}) async-start(), calls=%async_computation.15 | async-start | bytes 4456448 | tf_op jit(solution)/shard_map/all_gather | solution.py:241
  737.6 333.8 %all-gather.14.cloned.1.call-start = ((), (), s32[]{:S(2)}) async-start(), calls=%async_computation.13 | async-start | bytes 9748480 | tf_op jit(solution)/shard_map/all_gather | solution.py:240
  938.3 55.8 %copy-start.66 = (f32[128]{0:T(128)S(1)}, f32[128]{0:T(128)}, u32[]{:S(2)}) copy-start(f32[128]{0:T(128)} %copy-done.65) | copy-start | bytes 1540
  938.3 56.5 %copy-start.13 = (bf16[128,1024]{1,0:T(8,128)(2,1)S(1)}, bf16[128,1024]{1,0:T(8,128)(2,1)}, u32[]{:S(2)}) copy-start(bf16[128,1024]{1,0:T(8,128)(2,1)} %param.25) | copy-start | bytes 786436
  (109 other events, 651.7 us)
Sparse Core Ops, SparseCore 0:
  9.6 115.6 all-gather.7
  132.3 39.7 all-gather.9
  173.7 57.0 all-gather.11
  529.2 57.9 reduce-scatter.9
  590.0 147.4 reduce-scatter.7
  739.8 192.5 reduce-scatter.5
  934.6 56.0 all-gather.15
  993.0 78.3 all-gather.13
where the time goes:
time: 1100 us; the launch traced here: 1090 us
  waiting for transfers between devices  592 us (54%)
  matrix products  155 us (14%)
  local copies, waits for them, and re-layouts  116 us (11%)
  other arithmetic  111 us (10%)
  blocking collectives  70.2 us (6%)
  starting transfers between devices  31.6 us (3%)
  between operations  16.1 us (1%)
    reduce_scatter x1, waiting for transfers between devices, local(): lax.psum_scatter(in_grad, ('dp', 'seq'), scatter_dimension=0, tiled=True)  195 us
    reduce_scatter x1, waiting for transfers between devices, local(): lax.psum_scatter(out_grad, ('dp', 'seq'), scatter_dimension=0, tiled=True)  141 us
    all_gather x1, waiting for transfers between devices, local(): lax.all_gather(in_weight, 'dp', axis=0, tiled=True)  112 us
    all_gather x1, waiting for transfers between devices, local(): lax.all_gather(in_part, 'seq', axis=0, tiled=True)  75.6 us
    dot_general x24, matrix products, one_block(): inside = jnp.einsum('hts,shp->thp', weights, val_blk, precision=highest)  48.4 us
    psum x1, blocking collectives, local(): lax.psum((gain_grad, taps_grad, offset_grad, shift_grad, rates_grad, skip...  47 us
    another operation x50, other arithmetic  37.1 us
    dot_general x32, matrix products, one_block(): scores = jnp.dot(query_blk, key_blk.T, precision=highest)  31.6 us
  transfers between devices with their start and end apart: 14, of which 9 were waited for; matrix products, arithmetic and copies ran while one was open for 14% of the time, Pallas kernels for 0%

commit v1 on v0

--- a/solution.py
+++ b/solution.py
@@ -6,6 +6,17 @@
 BLOCK = 256
 epsilon = 1e-05
 highest = lax.Precision.HIGHEST
+
+
+def gather_around(x, axis, dim):
+    ways = lax.axis_size(axis)
+    pieces = [x]
+    for far in range(1, ways):
+        pieces.append(
+            lax.ppermute(pieces[far - 1], axis, [(d, (d - 1) % ways) for d in range(ways)])
+        )
+    line = jnp.concatenate(pieces, axis=dim)
+    return jnp.roll(line, lax.axis_index(axis) * x.shape[dim], axis=dim)
 
 
 def front_norm(values, gain):
@@ -237,7 +248,7 @@
         lax.psum_scatter(out_grad, ("dp", "seq"), scatter_dimension=0, tiled=True),
     )
     in_shard, out_shard = (
-        lax.all_gather(in_part, "seq", axis=0, tiled=True),
+        gather_around(in_part, "seq", 0),
         lax.all_gather(out_part, "seq", axis=0, tiled=True),
     )
     gain_all, taps_all, offset_all, shift_all, rates_all, skip_all, gate_all = lax.psum(

time: 1100 us -> 1060 us (0.964)
  waiting for transfers between devices: 592 us -> 466 us
  starting transfers between devices: 31.6 us -> 103 us
    reduce_scatter x1, waiting for transfers between devices: 141 us -> 0.02 us  [local(): lax.psum_scatter(out_grad, ('dp', 'seq'), scatter_dimension=0, tiled=True)]
    ppermute x0 -> x15, waiting for transfers between devices: none -> 107 us  [gather_around(): lax.ppermute(pieces[far - 1], axis, [(d, (d - 1) % ways) for d in range(w...]
    all_gather x1 -> x0, waiting for transfers between devices: 75.6 us -> none  [local(): lax.all_gather(in_part, 'seq', axis=0, tiled=True)]
    ppermute x0 -> x15, starting transfers between devices: none -> 72.1 us  [gather_around(): lax.ppermute(pieces[far - 1], axis, [(d, (d - 1) % ways) for d in range(w...]
    reduce_scatter x1, waiting for transfers between devices: 195 us -> 181 us  [local(): lax.psum_scatter(in_grad, ('dp', 'seq'), scatter_dimension=0, tiled=True)]
    unnamed x157 -> x178, local copies, waits for them, and re-layouts: 30.9 us -> 32.4 us
  transfers between devices with their start and end apart: 14 -> 28, of which waited for: 9 -> 22; matrix products, arithmetic and copies ran while one was open for 14% -> 33% of each run, Pallas kernels for 0% -> 0%
where the time goes in v1:
time: 1060 us; the launch traced here: 1050 us
  waiting for transfers between devices  466 us (44%)
  matrix products  163 us (15%)
  local copies, waits for them, and re-layouts  123 us (12%)
  other arithmetic  110 us (10%)
  starting transfers between devices  103 us (10%)
  blocking collectives  64.8 us (6%)
  between operations  16.2 us (2%)
    reduce_scatter x1, waiting for transfers between devices, local(): lax.psum_scatter(in_grad, ('dp', 'seq'), scatter_dimension=0, tiled=True)  181 us
    all_gather x1, waiting for transfers between devices, local(): lax.all_gather(in_weight, 'dp', axis=0, tiled=True)  112 us
    ppermute x15, waiting for transfers between devices, gather_around(): lax.ppermute(pieces[far - 1], axis, [(d, (d - 1) % ways) for d in range(w...  107 us
    ppermute x15, starting transfers between devices, gather_around(): lax.ppermute(pieces[far - 1], axis, [(d, (d - 1) % ways) for d in range(w...  72.1 us
    dot_general x24, matrix products, one_block(): inside = jnp.einsum('hts,shp->thp', weights, val_blk, precision=highest)  48.5 us
    psum x1, blocking collectives, local(): lax.psum((gain_grad, taps_grad, offset_grad, shift_grad, rates_grad, skip...  41.5 us
    another operation x50, other arithmetic  37.1 us
    unnamed x178, local copies, waits for them, and re-layouts  32.4 us
  transfers between devices with their start and end apart: 28, of which 22 were waited for; matrix products, arithmetic and copies ran while one was open for 33% of the time, Pallas kernels for 0%

profile of v1, /device:TPU:0, one launch (start us, length us, event | category | flops | bytes accessed | tf_op | source)
XLA Modules:
  0.0 1047.8 jit_solution(6792528382339815030)
XLA Ops:
  13.4 111.9 %all-gather.7.cloned.1.call-done = bf16[1024,4384]{0,1:T(8,128)(2,1)} async-done(((bf16[512,4384]{0,1:T(8,128)(2,1)}), bf16[1024,4384]{0,1:T(8,128)(2,1)}) %all-gather.7.cloned.1.call-update) | async-done | bytes 8978448 | tf_op jit(solution)/shard_map/all_gather | solution.py:130
  165.4 12.8 %all-to-all-done.1 = bf16[128,16,128]{2,0,1:T(8,128)(2,1)S(1)} async-done(((bf16[128,16,128]{2,0,1:T(8,128)(2,1)}), bf16[128,16,128]{2,0,1:T(8,128)(2,1)S(1)}, u32[]{:S(2)}, u32[]{:S(2)}) %all-to-all-start.1) | async-done | bytes 524320 | tf_op jit(solution)/shard_map/all_to_all | solution.py:155
  195.8 75.2 %while.44 = (s32[]{:T(128)}, f32[2,64,128]{2,1,0:T(8,128)S(1)}, f32[8,256,2,64]{1,3,2,0:T(8,128)}, f32[8,2,64,128]{3,2,1,0:T(8,128)}, f32[8,256,2]{1,2,0:T(2,128...) while((s32[]{:T(128)}, f32[2,64,128]{2,1,0:T(8,128)S(1)}, ...), condition=%wide.region_4.5_spmd.clone.clone, body=%wide.region_1.4_spmd.clone.clone.sunk | while | flops 302892544 | bytes 2142528 | solution.py:78
  289.9 10.1 all-to-all-done.2
  321.8 7.9 all-to-all-done.3
  341.9 179.1 %while.43 = (s32[]{:T(128)}, f32[2]{0:T(128)}, f32[2,64,128]{2,1,0:T(8,128)S(1)}, f32[8,256,2,64]{1,3,2,0:T(8,128)}, f32[8,256,2]{1,2,0:T(2,128)}, /*index=5*/f3...) while((s32[]{:T(128)}, f32[2]{0:T(128)}, ...), condition=%wide.region_20.21_spmd.clone, body=%wide.region_7.20_spmd.clone.sunk | while | flops 758179328 | bytes 7913312 | solution.py:78
  552.0 14.7 %all-to-all-done.4 = bf16[16,128,128]{2,1,0:T(8,128)(2,1)S(1)} async-done(((bf16[16,128,128]{2,1,0:T(8,128)(2,1)}), bf16[16,128,128]{2,1,0:T(8,128)(2,1)S(1)}, u32[]{:S(2)}, u32[]{:S(2)}) %all-to-all-start.4) | async-done | bytes 524320 | tf_op jit(solution)/shard_map/all_to_all | solution.py:217
  572.0 18.9 %reduce-scatter.10.cloned.1.call-done = bf16[128,256]{1,0:T(8,128)(2,1)} async-done(((bf16[2048,256]{1,0:T(8,128)(2,1)}), bf16[128,256]{1,0:T(8,128)(2,1)}) %reduce-scatter.10.cloned.1.call-update) | async-done | bytes 65552
  591.9 9.0 fusion.110
  612.4 41.5 %all-reduce.25 = (f32[1024]{0:T(1024)S(1)}, f32[4,2304]{1,0:T(4,128)S(1)}, f32[2304]{0:T(1024)S(1)}, f32[32]{0:T(128)S(1)}, f32[32]{0:T(128)S(1)}, /*index=5*/f32[32]{0:T(128)S(1)}, f32[2048]{0:T(1024)S(1)}) all-reduce(f32[1024]{0:T(1024)S(1)} %get-tuple-element.697, ...), channel_id=1, replica_groups=mesh['dp'=2,'seq'=16] {'dp','seq'}, use_global_device_ids=true, to_apply=%region_24.25 | all-reduce | flops 14688 | bytes 117504 | tf_op jit(solution)/shard_map/psum | solution.py:254
  659.3 181.4 %reduce-scatter.6.cloned.1.call-done = f32[32,4384]{1,0:T(8,128)} async-done(((f32[1024,4384]{1,0:T(8,128)}), f32[32,4384]{1,0:T(8,128)}) %reduce-scatter.6.cloned.1.call-update) | async-done | bytes 561168 | tf_op jit(solution)/shard_map/reduce_scatter | solution.py:247
  840.7 7.5 collective-permute-start
  860.2 7.2 collective-permute-done.1
  872.1 7.2 collective-permute-done.2
  883.9 7.2 collective-permute-done.3
  895.7 7.2 collective-permute-done.4
  907.6 7.2 collective-permute-done.5
  919.4 7.2 collective-permute-done.6
  931.2 7.2 collective-permute-done.7
  967.0 7.2 collective-permute-done.10
  978.8 7.2 collective-permute-done.11
  1002.5 7.2 collective-permute-done.13
  1014.3 7.2 collective-permute-done.14
  1026.4 9.4 copy.130
  (844 shorter events, 526.0 us)
Async XLA Ops:
  7.2 118.1 %all-gather.7.cloned.1.call-start = ((), (), s32[]{:S(2)}) async-start(), calls=%async_computation.9 | async-start | bytes 13467648 | tf_op jit(solution)/shard_map/all_gather | solution.py:130
  7.9 176.5 %all-gather.9.cloned.1.call-start = ((), (), s32[]{:S(2)}) async-start(), calls=%async_computation.10 | async-start | bytes 1114112 | tf_op jit(solution)/shard_map/all_gather | solution.py:158
  132.3 169.6 %all-gather.11.cloned.1.call-start = ((), (), s32[]{:S(2)}) async-start(), calls=%async_computation.11 | async-start | bytes 6291456 | tf_op jit(solution)/shard_map/all_gather | solution.py:137
  138.0 19.3 %all-to-all-start = ((bf16[128,16,2]{0,2,1:T(2,128)(2,1)}), bf16[128,16,2]{0,2,1:T(2,128)(2,1)S(1)}, u32[]{:S(2)}, u32[]{:S(2)}) async-start(bf16[128,16,2]{0,2,1:T(2,128)(2,1)} %bitcast.3), calls=%async_computation | async-start | bytes 16384 | tf_op jit(solution)/shard_map/all_to_all | solution.py:156
  157.3 21.0 %all-to-all-start.1 = ((bf16[128,16,128]{2,0,1:T(8,128)(2,1)}), bf16[128,16,128]{2,0,1:T(8,128)(2,1)S(1)}, u32[]{:S(2)}, u32[]{:S(2)}) async-start(bf16[128,16,128]{2,0,1:T(8,128)(2,1)} %copy.109), calls=%async_computation.1 | async-start | bytes 1048576 | tf_op jit(solution)/shard_map/all_to_all | solution.py:155
  280.5 19.5 %all-to-all-start.2 = ((bf16[16,128,128]{2,1,0:T(8,128)(2,1)}), bf16[16,128,128]{2,1,0:T(8,128)(2,1)S(1)}, u32[]{:S(2)}, u32[]{:S(2)}) async-start(bf16[16,128,128]{2,1,0:T(8,128)(2,1)} %bitcast.20), calls=%async_computation.2 | async-start | bytes 1048576 | tf_op jit(solution)/shard_map/all_to_all | solution.py:185
  311.1 18.6 %all-to-all-start.3 = ((bf16[128,16,128]{2,0,1:T(8,128)(2,1)}), bf16[128,16,128]{2,0,1:T(8,128)(2,1)S(1)}, u32[]{:S(2)}, u32[]{:S(2)}) async-start(bf16[128,16,128]{2,0,1:T(8,128)(2,1)} %copy.118), calls=%async_computation.3 | async-start | bytes 1048576 | tf_op jit(solution)/shard_map/all_to_all | solution.py:201
  315.2 219.3 %reduce-scatter.8.cloned.1.call-start = ((), (), s32[]{:S(2)}) async-start(), calls=%async_computation.13 | async-start | bytes 8650752 | tf_op jit(solution)/shard_map/reduce_scatter | solution.py:248
  321.6 269.3 %reduce-scatter.10.cloned.1.call-start = ((), (), s32[]{:S(2)}) async-start(), calls=%async_computation.15 | async-start | bytes 1114112
  534.2 125.1 %all-gather.13.cloned.1.call-start = ((), (), s32[]{:S(2)}) async-start(), calls=%async_computation.14 | async-start | bytes 4456448 | tf_op jit(solution)/shard_map/all_gather | solution.py:252
  547.1 19.6 %all-to-all-start.4 = ((bf16[16,128,128]{2,1,0:T(8,128)(2,1)}), bf16[16,128,128]{2,1,0:T(8,128)(2,1)S(1)}, u32[]{:S(2)}, u32[]{:S(2)}) async-start(bf16[16,128,128]{2,1,0:T(8,128)(2,1)} %bitcast.441), calls=%async_computation.4 | async-start | bytes 1048576 | tf_op jit(solution)/shard_map/all_to_all | solution.py:217
  566.7 25.2 %all-to-all-start.5 = ((bf16[16,128,2]{1,2,0:T(2,128)(2,1)}), bf16[16,128,2]{1,2,0:T(2,128)(2,1)S(1)}, u32[]{:S(2)}, u32[]{:S(2)}) async-start(bf16[16,128,2]{1,2,0:T(2,128)(2,1)} %fusion.124), calls=%async_computation.5 | async-start | bytes 16384 | tf_op jit(solution)/shard_map/all_to_all | solution.py:220
  571.6 269.0 %reduce-scatter.6.cloned.1.call-start = ((), (), s32[]{:S(2)}) async-start(), calls=%async_computation.12 | async-start | bytes 18923520 | tf_op jit(solution)/shard_map/reduce_scatter | solution.py:247
  840.7 15.0 %collective-permute-start = (f32[32,4384]{1,0:T(8,128)}, f32[32,4384]{1,0:T(8,128)S(1)}, u32[]{:S(2)}, u32[]{:S(2)}) collective-permute-start(f32[32,4384]{1,0:T(8,128)} %reduce-scatter.6.cloned.1.call-done), channel_id=1, source_target_pairs={{0,15},{1,0},{2,1},{3,2},{4,3},{5,4},{6,5},{7,6},{8,7},{9,8},{10,9... | collective-permute-start | bytes 1683464 | tf_op jit(solution)/shard_map/ppermute | solution.py:16
  867.4 11.8 %collective-permute-start.2 = (f32[32,4384]{1,0:T(8,128)S(1)}, f32[32,4384]{1,0:T(8,128)S(1)}, u32[]{:S(2)}, u32[]{:S(2)}) collective-permute-start(f32[32,4384]{1,0:T(8,128)S(1)} %collective-permute-done.1), channel_id=1, source_target_pairs={{0,15},{1,0},{2,1},{3,2},{4,3},{5,4},{6,5},{7,6},{8,7},{9,8},{10,9... | collective-permute-start | bytes 1683464 | tf_op jit(solution)/shard_map/ppermute | solution.py:16
  879.2 11.8 %collective-permute-start.3 = (f32[32,4384]{1,0:T(8,128)S(1)}, f32[32,4384]{1,0:T(8,128)S(1)}, u32[]{:S(2)}, u32[]{:S(2)}) collective-permute-start(f32[32,4384]{1,0:T(8,128)S(1)} %collective-permute-done.2), channel_id=1, source_target_pairs={{0,15},{1,0},{2,1},{3,2},{4,3},{5,4},{6,5},{7,6},{8,7},{9,8},{10,9... | collective-permute-start | bytes 1683464 | tf_op jit(solution)/shard_map/ppermute | solution.py:16
  891.1 11.8 %collective-permute-start.4 = (f32[32,4384]{1,0:T(8,128)S(1)}, f32[32,4384]{1,0:T(8,128)S(1)}, u32[]{:S(2)}, u32[]{:S(2)}) collective-permute-start(f32[32,4384]{1,0:T(8,128)S(1)} %collective-permute-done.3), channel_id=1, source_target_pairs={{0,15},{1,0},{2,1},{3,2},{4,3},{5,4},{6,5},{7,6},{8,7},{9,8},{10,9... | collective-permute-start | bytes 1683464 | tf_op jit(solution)/shard_map/ppermute | solution.py:16
  902.9 11.8 %collective-permute-start.5 = (f32[32,4384]{1,0:T(8,128)S(1)}, f32[32,4384]{1,0:T(8,128)S(1)}, u32[]{:S(2)}, u32[]{:S(2)}) collective-permute-start(f32[32,4384]{1,0:T(8,128)S(1)} %collective-permute-done.4), channel_id=1, source_target_pairs={{0,15},{1,0},{2,1},{3,2},{4,3},{5,4},{6,5},{7,6},{8,7},{9,8},{10,9... | collective-permute-start | bytes 1683464 | tf_op jit(solution)/shard_map/ppermute | solution.py:16
  914.7 11.8 %collective-permute-start.6 = (f32[32,4384]{1,0:T(8,128)S(1)}, f32[32,4384]{1,0:T(8,128)S(1)}, u32[]{:S(2)}, u32[]{:S(2)}) collective-permute-start(f32[32,4384]{1,0:T(8,128)S(1)} %collective-permute-done.5), channel_id=1, source_target_pairs={{0,15},{1,0},{2,1},{3,2},{4,3},{5,4},{6,5},{7,6},{8,7},{9,8},{10,9... | collective-permute-start | bytes 1683464 | tf_op jit(solution)/shard_map/ppermute | solution.py:16
  926.6 11.8 %collective-permute-start.7 = (f32[32,4384]{1,0:T(8,128)S(1)}, f32[32,4384]{1,0:T(8,128)S(1)}, u32[]{:S(2)}, u32[]{:S(2)}) collective-permute-start(f32[32,4384]{1,0:T(8,128)S(1)} %collective-permute-done.6), channel_id=1, source_target_pairs={{0,15},{1,0},{2,1},{3,2},{4,3},{5,4},{6,5},{7,6},{8,7},{9,8},{10,9... | collective-permute-start | bytes 1683464 | tf_op jit(solution)/shard_map/ppermute | solution.py:16
  938.4 12.1 %collective-permute-start.8 = (f32[32,4384]{1,0:T(8,128)S(1)}, f32[32,4384]{1,0:T(8,128)S(1)}, u32[]{:S(2)}, u32[]{:S(2)}) collective-permute-start(f32[32,4384]{1,0:T(8,128)S(1)} %collective-permute-done.7), channel_id=1, source_target_pairs={{0,15},{1,0},{2,1},{3,2},{4,3},{5,4},{6,5},{7,6},{8,7},{9,8},{10,9... | collective-permute-start | bytes 1683464 | tf_op jit(solution)/shard_map/ppermute | solution.py:16
  950.5 11.8 %collective-permute-start.9 = (f32[32,4384]{1,0:T(8,128)S(1)}, f32[32,4384]{1,0:T(8,128)S(1)}, u32[]{:S(2)}, u32[]{:S(2)}) collective-permute-start(f32[32,4384]{1,0:T(8,128)S(1)} %collective-permute-done.8), channel_id=1, source_target_pairs={{0,15},{1,0},{2,1},{3,2},{4,3},{5,4},{6,5},{7,6},{8,7},{9,8},{10,9... | collective-permute-start | bytes 1683464 | tf_op jit(solution)/shard_map/ppermute | solution.py:16
  962.3 11.8 %collective-permute-start.10 = (f32[32,4384]{1,0:T(8,128)S(1)}, f32[32,4384]{1,0:T(8,128)S(1)}, u32[]{:S(2)}, u32[]{:S(2)}) collective-permute-start(f32[32,4384]{1,0:T(8,128)S(1)} %collective-permute-done.9), channel_id=1, source_target_pairs={{0,15},{1,0},{2,1},{3,2},{4,3},{5,4},{6,5},{7,6},{8,7},{9,8},{10,9... | collective-permute-start | bytes 1683464 | tf_op jit(solution)/shard_map/ppermute | solution.py:16
  974.2 11.8 %collective-permute-start.11 = (f32[32,4384]{1,0:T(8,128)S(1)}, f32[32,4384]{1,0:T(8,128)S(1)}, u32[]{:S(2)}, u32[]{:S(2)}) collective-permute-start(f32[32,4384]{1,0:T(8,128)S(1)} %collective-permute-done.10), channel_id=1, source_target_pairs={{0,15},{1,0},{2,1},{3,2},{4,3},{5,4},{6,5},{7,6},{8,7},{9,8},{10,9... | collective-permute-start | bytes 1683464 | tf_op jit(solution)/shard_map/ppermute | solution.py:16
  (110 other events, 1421.3 us)
Sparse Core Ops, SparseCore 0:
  9.6 115.6 all-gather.6
  132.4 39.6 all-gather.8
  173.7 57.0 all-gather.10
  321.7 148.8 reduce-scatter.7
  534.3 56.5 reduce-scatter.9
  593.1 50.4 all-gather.12
  646.0 194.6 reduce-scatter.5
